TPU v7x, 512 devices: a whole 4x8x8 slice. The times are simulated.
512 devices in a mesh: dp: 4 (over x), tensor: 128 (over z, y, core).
Axes of the slice: x: 4, y: 8, z: 8, core: 2. Of those that a mesh axis runs over, the one named last changes fastest.
Arguments:
- hidden: bfloat16 [8192, 2048], P(('dp', 'tensor')), may hold values from -6 to 6
- norm_gain: float32 [2048], replicated, may hold values from 0.5 to 1.5
- head_weight: bfloat16 [2048, 102400], P('dp', 'tensor'), as said below
- token_ids: int32 [8192], P(('dp', 'tensor')), may hold values from 0 to 102399
- lengths: int32 [4, 4], P('dp'), may hold values from 1 to 512, 1024 in all within a row
Outputs:
- logprob: float32 [8192], P(('dp', 'tensor'))
- entropy: float32 [8192], P(('dp', 'tensor'))
Inputs may be any that keep to these rules, and one draw needn't show every extreme that they name: Each index of dp has 4 lengths that sum to exactly 1024, and one of them equals 512. `head_weight`: head weights.
All inputs are finite; a program needn't handle non-finite values.
Results may differ from a plain program's by a relative error of at most 0.0045.
Values may be sent and summed in bfloat16 or wider, within the bound.
No kernel may reach another device: no remote copies, remote signals or barrier semaphores. Data moves between devices by JAX's collectives and lax.ppermute only.
A program may use at most 64 MiB of HBM per device.

v0:
```python
import jax
import jax.numpy as jnp
from jax import lax
from jax.sharding import PartitionSpec as P

SEQ_DP = 4
SLOT = 512


def per_device(hidden, norm_gain, head_weight, token_ids, lengths):
    row_dev = hidden.shape[0]
    tensor_idx = lax.axis_index("tensor")
    wide = hidden.astype(jnp.float32)
    meansq = jnp.mean(wide * wide, axis=-1, keepdims=True)
    normed = (wide * lax.rsqrt(meansq + 1e-06) * norm_gain).astype(jnp.bfloat16)
    weight = lax.all_gather(head_weight, "dp", axis=0, tiled=True)
    vocab_dev = weight.shape[1]
    vstart = tensor_idx * vocab_dev
    seq_len = lengths[0]
    seq_iota = jnp.arange(SEQ_DP, dtype=jnp.int32)
    vocab_iota = jnp.arange(vocab_dev, dtype=jnp.int32)
    own_rows = tensor_idx * row_dev + jnp.arange(row_dev, dtype=jnp.int32)
    logits = jnp.dot(
        lax.all_gather(normed, "tensor", axis=0, tiled=True),
        weight,
        preferred_element_type=jnp.float32,
    )
    top = jnp.max(logits, axis=1)
    expo = jnp.exp(logits - top[:, None])
    total = jnp.sum(expo, axis=1)
    moment = jnp.sum(expo * logits, axis=1)
    hit = (lax.all_gather(token_ids, "tensor", axis=0, tiled=True) - vstart)[:, None] == vocab_iota[
        None, :
    ]
    chosen = jnp.sum(jnp.where(hit, logits, 0.0), axis=1)
    fresh = (top, total, moment, chosen)
    top, total, moment, chosen = tuple((new for new in fresh))
    onehot = (own_rows // SLOT)[:, None] == seq_iota[None, :]
    length_of = jnp.sum(jnp.where(onehot, seq_len[None, :], 0), axis=1)
    within = own_rows % SLOT
    scored = within < length_of
    top_all = lax.pmax(top, "tensor")
    rescale = jnp.exp(top - top_all)
    top_own = top_all[own_rows]
    total_all, moment_all, chosen_all = lax.psum(
        (total * rescale, moment * rescale, chosen), "tensor"
    )
    total_own, moment_own, chosen_own = (
        total_all[own_rows],
        moment_all[own_rows],
        chosen_all[own_rows],
    )
    safe_total = jnp.where(scored, total_own, 1.0)
    lse = top_own + jnp.log(safe_total)
    logprob = jnp.where(scored, chosen_own - lse, 0.0)
    entropy = jnp.where(scored, lse - moment_own / safe_total, 0.0)
    return (logprob, entropy)


def solution(mesh):
    return jax.shard_map(
        per_device,
        mesh=mesh,
        in_specs=(
            P(("dp", "tensor"), None),
            P(),
            P("dp", "tensor"),
            P(("dp", "tensor")),
            P("dp", None),
        ),
        out_specs=(P(("dp", "tensor")), P(("dp", "tensor"))),
        check_vma=False,
    )
```

profile of v0, /device:TPU:2, one launch (start us, length us, event | category | flops | bytes accessed | tf_op | source)
XLA Modules:
  0.0 923.0 jit_solution(2070822759771183285)
XLA Ops:
  7.2 0.0 all-gather.5.cloned.1.call-start
  7.2 0.7 all-gather.5.cloned.1.call-update
  7.9 0.0 all-gather.3.cloned.1.call-start
  7.9 1.0 fusion.1
  8.9 1.6 fusion.3
  10.5 0.0 all-gather.3.cloned.1.call-update
  10.5 1.3 dynamic-slice
  12.5 0.9 dynamic-update-slice
  13.3 32.3 %all-reduce = s32[2048]{0:T(1024)S(1)} all-reduce(s32[2048]{0:T(1024)S(1)} %dynamic-update-slice), channel_id=1, replica_groups=mesh['dp'=4,'tensor'=128] {'tensor'}, use_global_device_ids=true, to_apply=%add | all-reduce | flops 2048 | bytes 16384
  45.6 0.7 select_reduce_fusion.1
  46.4 13.6 %all-gather.5.cloned.1.call-done = bf16[2048,800]{0,1:T(8,128)(2,1)} async-done(((bf16[512,800]{0,1:T(8,128)(2,1)}), bf16[2048,800]{0,1:T(8,128)(2,1)}) %all-gather.5.cloned.1.call-update) | async-done | bytes 3276816 | tf_op jit(solution)/shard_map/all_gather | solution.py:16
  60.0 92.3 %all-gather.3.cloned.1.call-done = bf16[2048,2048]{1,0:T(8,128)(2,1)} async-done(((bf16[16,2048]{1,0:T(8,128)(2,1)}), bf16[2048,2048]{1,0:T(8,128)(2,1)}) %all-gather.3.cloned.1.call-update) | async-done | bytes 8388624 | tf_op jit(solution)/shard_map/all_gather | solution.py:24
  152.3 12.1 %fusion.8 = (f32[2048]{0:T(1024)S(1)}, f32[2048,800]{0,1:T(8,128)}) fusion(bf16[2048,2048]{1,0:T(8,128)(2,1)} %all-gather.3.cloned.1.call-done, bf16[2048,800]{0,1:T(8,128)(2,1)} %all-gather.5.cloned.1.call-done), kind=kOutput, calls=%fused_computation.35 | convolution fusion | flops 6712522752 | bytes 18227200 | tf_op jit(solution)/shard_map/dot_general | solution.py:23
  164.3 253.6 %pmax.7 = f32[2048]{0:T(1024)S(1)} all-reduce(f32[2048]{0:T(1024)S(1)} %get-tuple-element.12), channel_id=1, replica_groups=mesh['dp'=4,'tensor'=128] {'tensor'}, use_global_device_ids=true, to_apply=%region_5.6 | all-reduce | flops 2048 | bytes 16384 | tf_op jit(solution)/shard_map/pmax | solution.py:42
  417.9 4.1 multiply_reduce_fusion
  422.0 0.7 gather_fusion.1
  422.7 490.9 %all-reduce.1 = (f32[2048]{0:T(1024)S(1)}, f32[2048]{0:T(1024)S(1)}, f32[2048]{0:T(1024)S(1)}) all-reduce(f32[2048]{0:T(1024)S(1)} %get-tuple-element.4, f32[2048]{0:T(1024)S(1)} %get-tuple-element.9, f32[2048]{0:T(1024)S(1)} %get-tuple-element.8), channel_id=1, replica_groups=mesh['dp'=4,'tensor'=128] {'tensor'}, use_global_device_ids=true, to_apply=%region_3.0 | all-reduce | flops 6144 | bytes 49152 | tf_op jit(solution)/shard_map/psum | solution.py:45
  913.6 0.7 gather_fusion
  914.3 0.7 gather_fusion.2
  914.9 0.7 gather_fusion.3
  915.6 0.5 subtract_select_fusion
  (7 shorter events, 0.0 us)
Async XLA Ops:
  7.2 52.8 %all-gather.5.cloned.1.call-start = ((), (), s32[]{:S(2)}) async-start(), calls=%async_computation.1 | async-start | bytes 4096000 | tf_op jit(solution)/shard_map/all_gather | solution.py:16
  7.9 144.4 %all-gather.3.cloned.1.call-start = ((), (), s32[]{:S(2)}) async-start(), calls=%async_computation | async-start | bytes 8454144 | tf_op jit(solution)/shard_map/all_gather | solution.py:24
Sparse Core Ops, SparseCore 0:
  10.1 49.8 all-gather.4
  63.1 89.1 all-gather.2
where the time goes:
time: 923 us
  blocking collectives  777 us (84%)
  waiting for transfers between devices  107 us (12%)
  between operations  14.7 us (2%)
  matrix products  12.1 us (1%)
    psum x1, blocking collectives, per_device(): lax.psum((total * rescale, moment * rescale, chosen), 'tensor')  491 us
    pmax x1, blocking collectives, per_device(): top_all = lax.pmax(top, 'tensor')  254 us
    all_gather x1, waiting for transfers between devices, per_device(): lax.all_gather(normed, 'tensor', axis=0, tiled=True)  92.3 us
    unnamed x1, blocking collectives  32.3 us
  transfers between devices with their start and end apart: 2, of which 2 were waited for; matrix products, arithmetic and copies ran while one was open for 1% of the time, Pallas kernels for 0%

commit v1 on v0

--- a/solution.py
+++ b/solution.py
@@ -21,7 +21,9 @@
     vocab_iota = jnp.arange(vocab_dev, dtype=jnp.int32)
     own_rows = tensor_idx * row_dev + jnp.arange(row_dev, dtype=jnp.int32)
     logits = jnp.dot(
-        lax.all_gather(normed, "tensor", axis=0, tiled=True),
+        jnp.concatenate(
+            lax.all_to_all(jnp.stack([normed] * lax.axis_size("tensor")), "tensor", 0, 0), axis=0
+        ),
         weight,
         preferred_element_type=jnp.float32,
     )

time: 923 us -> 1070 us (1.16)
  blocking collectives: 777 us -> 1010 us
  waiting for transfers between devices: 107 us -> 0.7 us
  starting transfers between devices: 0.08 us -> 18.5 us
    unnamed x1, blocking collectives: 32.3 us -> 250 us
    all_gather x1 -> x0, waiting for transfers between devices: 92.3 us -> none  [per_device(): lax.all_gather(normed, 'tensor', axis=0, tiled=True)]
    all_to_all x0 -> x1, starting transfers between devices: none -> 18.5 us  [per_device(): lax.all_to_all(jnp.stack([normed] * lax.axis_size('tensor')), 'tensor', 0...]
    all_gather x1, waiting for transfers between devices: 13.6 us -> 0.02 us  [per_device(): weight = lax.all_gather(head_weight, 'dp', axis=0, tiled=True)]
    pmax x1, blocking collectives: 254 us -> 265 us  [per_device(): top_all = lax.pmax(top, 'tensor')]
  transfers between devices with their start and end apart: 2 -> 2, of which waited for: 2 -> 0; matrix products, arithmetic and copies ran while one was open for 1% -> 0% of each run, Pallas kernels for 0% -> 0%
where the time goes in v1:
time: 1070 us
  blocking collectives  1010 us (94%)
  starting transfers between devices  18.5 us (2%)
  between operations  14.8 us (1%)
  matrix products  12.1 us (1%)
    psum x1, blocking collectives, per_device(): lax.psum((total * rescale, moment * rescale, chosen), 'tensor')  491 us
    pmax x1, blocking collectives, per_device(): top_all = lax.pmax(top, 'tensor')  265 us
    unnamed x1, blocking collectives  250 us
  transfers between devices with their start and end apart: 2, of which 0 were waited for; matrix products, arithmetic and copies ran while one was open for 0% of the time, Pallas kernels for 0%

profile of v1, /device:TPU:2, one launch (start us, length us, event | category | flops | bytes accessed | tf_op | source)
XLA Modules:
  0.0 1067.5 jit_solution(5954348087897906832)
XLA Ops:
  7.2 1.0 fusion.1
  8.1 0.9 fusion.3
  9.1 4.3 stack.2
  13.3 0.0 copy-start
  13.4 0.0 copy-start.1
  13.4 18.5 %all-to-all-start = ((bf16[128,16,2048]{2,1,0:T(8,128)(2,1)}), bf16[128,16,2048]{2,1,0:T(8,128)(2,1)}, u32[]{:S(2)}, u32[]{:S(2)}) async-start(bf16[128,16,2048]{2,1,0:T(8,128)(2,1)} %stack.2), calls=%async_computation | async-start | bytes 16777216 | tf_op jit(solution)/shard_map/all_to_all | solution.py:25
  31.8 0.0 all-gather.2.cloned.1.call-start
  31.9 0.7 all-gather.2.cloned.1.call-update
  32.6 1.3 dynamic-slice
  34.5 0.0 copy-done
  34.5 0.3 dynamic-update-slice
  34.8 250.1 %all-reduce = s32[2048]{0:T(1024)S(1)} all-reduce(s32[2048]{0:T(1024)S(1)} %dynamic-update-slice), channel_id=1, replica_groups=mesh['dp'=4,'tensor'=128] {'tensor'}, use_global_device_ids=true, to_apply=%add | all-reduce | flops 2048 | bytes 16384
  284.9 0.0 copy-done.1
  284.9 0.1 select_reduce_fusion.1
  285.0 0.0 all-gather.2.cloned.1.call-done
  285.0 0.0 all-to-all-done
  285.1 12.1 %fusion.8 = (f32[2048]{0:T(1024)S(1)}, f32[2048,800]{0,1:T(8,128)}) fusion(bf16[2048,2048]{1,0:T(8,128)(2,1)} %bitcast.2, bf16[2048,800]{0,1:T(8,128)(2,1)} %all-gather.2.cloned.1.call-done), kind=kOutput, calls=%fused_computation.35 | convolution fusion | flops 6712522752 | bytes 18227200 | tf_op jit(solution)/shard_map/dot_general | solution.py:23
  297.1 265.4 %pmax.7 = f32[2048]{0:T(1024)S(1)} all-reduce(f32[2048]{0:T(1024)S(1)} %get-tuple-element.12), channel_id=1, replica_groups=mesh['dp'=4,'tensor'=128] {'tensor'}, use_global_device_ids=true, to_apply=%region_5.6 | all-reduce | flops 2048 | bytes 16384 | tf_op jit(solution)/shard_map/pmax | solution.py:44
  562.5 4.1 multiply_reduce_fusion
  566.6 0.7 gather_fusion.1
  567.3 490.9 %all-reduce.1 = (f32[2048]{0:T(1024)S(1)}, f32[2048]{0:T(1024)S(1)}, f32[2048]{0:T(1024)S(1)}) all-reduce(f32[2048]{0:T(1024)S(1)} %get-tuple-element.4, f32[2048]{0:T(1024)S(1)} %get-tuple-element.9, f32[2048]{0:T(1024)S(1)} %get-tuple-element.8), channel_id=1, replica_groups=mesh['dp'=4,'tensor'=128] {'tensor'}, use_global_device_ids=true, to_apply=%region_3.0 | all-reduce | flops 6144 | bytes 49152 | tf_op jit(solution)/shard_map/psum | solution.py:47
  1058.2 0.7 gather_fusion
  1058.8 0.7 gather_fusion.2
  1059.5 0.7 gather_fusion.3
  1060.1 0.5 subtract_select_fusion
  (7 shorter events, 0.0 us)
Async XLA Ops:
  13.3 21.2 %copy-start = (s32[16]{0:T(128)S(1)}, s32[16]{0:T(128)}, u32[]{:S(2)}) copy-start(s32[16]{0:T(128)} %param.8) | copy-start | bytes 196
  13.4 271.6 %copy-start.1 = (s32[1,4]{1,0:T(1,128)S(1)}, s32[1,4]{1,0:T(1,128)}, u32[]{:S(2)}) copy-start(s32[1,4]{1,0:T(1,128)} %param.9) | copy-start | bytes 52
  13.4 271.7 %all-to-all-start = ((bf16[128,16,2048]{2,1,0:T(8,128)(2,1)}), bf16[128,16,2048]{2,1,0:T(8,128)(2,1)}, u32[]{:S(2)}, u32[]{:S(2)}) async-start(bf16[128,16,2048]{2,1,0:T(8,128)(2,1)} %stack.2), calls=%async_computation | async-start | bytes 16777216 | tf_op jit(solution)/shard_map/all_to_all | solution.py:25
  31.8 253.2 %all-gather.2.cloned.1.call-start = ((), (), s32[]{:S(2)}) async-start(), calls=%async_computation.1 | async-start | bytes 4096000 | tf_op jit(solution)/shard_map/all_gather | solution.py:16
Sparse Core Ops, SparseCore 0:
  34.8 45.6 all-gather.1
